TPU v7x, 32 devices: a whole 2x2x4 slice. The times are simulated.
32 devices in a mesh: groups: 2 (over y), expert: 4 (over z), tensor: 4 (over x, core).
Axes of the slice: x: 2, y: 2, z: 4, core: 2. Of those that a mesh axis runs over, the one named last changes fastest.
Arguments:
- tokens: bfloat16 [1024, 4096], P(('groups', 'expert'), 'tensor'), parts along dimension 0, may hold values from -130 to 130
- norm_gain: float32 [4096], replicated, may hold values from 0.5 to 1.5
- router: bfloat16 [4096, 8], replicated, may hold values from -0.09375 to 0.09375
- expert_ids: int32 [1024, 2], P(('groups', 'expert')), parts along dimension 0, may hold values from 0 to 7, all different within a row; in each aligned block of 128 rows (0 to 127, 128 to 255, ...) at most 40 rows name the same one
- w_gate: bfloat16 [4, 2, 4096, 7168], P('expert', None, None, 'tensor'), may hold values from -0.09375 to 0.09375
- w_down: bfloat16 [4, 2, 7168, 4096], P('expert', None, None, 'tensor'), may hold values from -0.0625 to 0.0625
Outputs:
- mixed: bfloat16 [1024, 4096], P(('groups', 'expert'), 'tensor'), parts along dimension 0
There are 2 independent parts, one for each index of `groups`. A program takes and returns all parts, laid end to end along the dimension named above; an argument that names none is the same for every part. Nothing has to cross between parts.
Inputs may be any that keep to these rules, and one draw needn't show every extreme that they name: `expert_ids`: each row names two different experts; within each aligned block of 128 rows (the tokens of one index of the expert axis) no expert is named by more than 40 rows, a bound that some block reaches.
All inputs are finite; a program needn't handle non-finite values.
Results may differ from a plain program's by a relative error of at most 0.0085.
Values may be sent and summed in bfloat16 or wider, within the bound.
A program may use at most 128 MiB of HBM per device.

v0:
```python
import jax
import jax.numpy as jnp
from jax import lax
from jax.sharding import PartitionSpec as P

CAP = 40


epsilon = 1e-05


def expert_slots(expert_ids, experts, capacity):
    flat_ids = expert_ids.reshape(-1)
    onehot = (flat_ids[:, None] == jnp.arange(experts, dtype=jnp.int32)[None, :]).astype(jnp.int32)
    before = jnp.cumsum(onehot, axis=0) - onehot
    slot_index = jnp.sum(before * onehot, axis=1)
    return (flat_ids * capacity + slot_index).reshape(expert_ids.shape)


def gate_pair(logits, expert_ids):
    labels = jnp.arange(logits.shape[1], dtype=jnp.int32)
    picked = (expert_ids[:, :, None] == labels[None, None, :]).astype(jnp.float32)
    chosen = jnp.sum(picked * logits[:, None, :], axis=2)
    first_gate = 1.0 / (1.0 + jnp.exp(chosen[:, 1] - chosen[:, 0]))
    second_gate = 1.0 / (1.0 + jnp.exp(chosen[:, 0] - chosen[:, 1]))
    return jnp.stack([first_gate, second_gate], axis=1).astype(jnp.bfloat16)


def on_device(tokens, norm_gain, router, expert_ids, w_gate, w_down):
    tok_rows = tokens.shape[0]
    experts = router.shape[1]
    devices = lax.axis_size("expert")
    local_count = w_gate.shape[1]
    pieces = max(1, devices // experts)
    feature_width = tokens.shape[1]
    first_col = lax.axis_index("tensor") * feature_width
    gain_part = lax.dynamic_slice_in_dim(norm_gain, first_col, feature_width, 0)
    router_part = lax.dynamic_slice_in_dim(router, first_col, feature_width, 0)
    values = tokens.astype(jnp.float32)
    squares_sum = lax.psum(jnp.sum(values * values, axis=1), "tensor")
    inverse_rms = lax.rsqrt(squares_sum[:, None] / norm_gain.shape[0] + epsilon)
    normed = (values * inverse_rms * gain_part[None, :]).astype(jnp.bfloat16)
    logit_terms = jnp.dot(normed, router_part, preferred_element_type=jnp.float32)
    logits = lax.psum(logit_terms, "tensor")
    gate_values = gate_pair(logits, expert_ids)
    slot_place = expert_slots(expert_ids, experts, CAP)
    slot_rows = jnp.arange(experts * CAP, dtype=jnp.int32)
    matches = slot_rows[:, None, None] == slot_place[None, :, :]
    dispatch = jnp.any(matches, axis=2).astype(jnp.bfloat16)
    buffer = jnp.dot(dispatch, normed, preferred_element_type=jnp.float32).astype(jnp.bfloat16)
    buffer = buffer.reshape(experts, CAP, buffer.shape[1])
    buffer = jnp.repeat(buffer, pieces, axis=0).reshape(devices, local_count, CAP, buffer.shape[2])
    received = lax.all_to_all(buffer, "expert", split_axis=0, concat_axis=0, tiled=True)
    received = lax.all_gather(received, "tensor", axis=3, tiled=True)
    gate_terms = jnp.einsum(
        "glcd,ldf->glcf", received, w_gate[0], preferred_element_type=jnp.float32
    )
    hidden = jax.nn.silu(gate_terms).astype(jnp.bfloat16)
    hidden = lax.all_gather(hidden, "tensor", axis=3, tiled=True)
    partial_value = jnp.einsum(
        "glcf,lfd->glcd", hidden, w_down[0], preferred_element_type=jnp.float32
    ).astype(jnp.bfloat16)
    returned = lax.all_to_all(partial_value, "expert", split_axis=0, concat_axis=0, tiled=True)
    slot_index = slot_place - expert_ids * CAP
    owner = expert_ids // local_count
    within = expert_ids - owner * local_count
    piece_ids = jnp.arange(pieces, dtype=jnp.int32)[None, None, :]
    target = (
        (owner[:, :, None] * pieces + piece_ids) * local_count + within[:, :, None]
    ) * CAP + slot_index[:, :, None]
    target = target.reshape(tok_rows, -1)
    weights = jnp.repeat(gate_values, pieces, axis=1).astype(jnp.float32)
    total_rows = devices * local_count * CAP
    columns = jnp.arange(total_rows, dtype=jnp.int32)
    combine = jnp.sum(
        jnp.where(columns[None, :, None] == target[:, None, :], weights[:, None, :], 0.0), axis=2
    ).astype(jnp.bfloat16)
    mixed = jnp.dot(
        combine, returned.reshape(total_rows, returned.shape[3]), preferred_element_type=jnp.float32
    )
    return mixed.astype(jnp.bfloat16)


def solution(mesh):
    return jax.shard_map(
        on_device,
        mesh=mesh,
        in_specs=(
            P(("groups", "expert"), "tensor"),
            P(),
            P(),
            P(("groups", "expert"), None),
            P("expert", None, None, "tensor"),
            P("expert", None, None, "tensor"),
        ),
        out_specs=P(("groups", "expert"), "tensor"),
        check_vma=False,
    )
```

profile of v0, /device:TPU:0, one launch (start us, length us, event | category | flops | bytes accessed | tf_op | source)
XLA Modules:
  0.0 167.4 jit_solution(11675938504098203109)
XLA Ops:
  6.5 0.0 copy-start
  6.5 0.0 all-gather.3.cloned.1.call-start
  6.5 0.8 copy.37
  7.4 0.1 eq.69
  7.5 0.1 eq.65
  7.7 0.6 reduce-window.6
  8.2 0.2 slice_reduce_fusion
  8.5 0.1 fusion.25
  8.6 0.1 reduce_sum.39
  8.7 0.1 copy.39
  8.8 0.7 multiply_add_fusion
  9.6 1.1 fusion.15
  10.6 8.4 %psum.14 = f32[128]{0:T(128)S(1)} all-reduce(f32[128]{0:T(128)S(1)} %fusion.15), channel_id=1, replica_groups=mesh['groups'=2,'expert'=4,'tensor'=4] {'tensor'}, use_global_device_ids=true, to_apply=%region_4.0 | all-reduce | flops 128 | bytes 1024 | tf_op jit(solution)/shard_map/psum | solution.py:40
  19.0 0.7 dynamic_slice.6
  19.7 1.4 convolution_convert_fusion
  21.1 20.8 %all_to_all.10 = bf16[4,2,40,1024]{3,2,1,0:T(8,128)(2,1)S(1)} all-to-all(bf16[4,2,40,1024]{3,2,1,0:T(8,128)(2,1)S(1)} %bitcast.42), channel_id=1, replica_groups=mesh['groups'=2,'expert'=4,'tensor'=4] {'expert'}, dimensions={0} | all-to-all | bytes 1310720 | tf_op jit(solution)/shard_map/all_to_all | solution.py:53
  41.8 0.9 copy.40
  42.7 0.0 all-gather.3.cloned.1.call-update
  42.8 0.0 all-gather.5.cloned.1.call-start
  42.8 24.8 %all-gather.3.cloned.1.call-done = bf16[4,2,40,4096]{3,2,0,1:T(8,128)(2,1)} async-done(((bf16[4,2,40,1024]{3,2,0,1:T(8,128)(2,1)}), bf16[4,2,40,4096]{3,2,0,1:T(8,128)(2,1)}) %all-gather.3.cloned.1.call-update) | async-done | bytes 2621456 | tf_op jit(solution)/shard_map/all_gather | solution.py:54
  67.6 16.3 %multiply_convert_fusion = bf16[4,2,40,1792]{3,2,0,1:T(8,128)(2,1)} fusion(bf16[4,2,40,4096]{3,2,0,1:T(8,128)(2,1)} %all-gather.3.cloned.1.call-done, bf16[1,2,4096,1792]{3,2,1,0:T(8,128)(2,1)} %param.10), kind=kOutput, calls=%fused_computation.5 | convolution fusion | flops 4700487680 | bytes 33128448 | tf_op jit(solution)/shard_map/glcd,ldf->glcf/dot_general | solution.py:55
  83.8 0.0 all-gather.5.cloned.1.call-update
  83.9 36.8 %all-gather.5.cloned.1.call-done = bf16[4,2,40,7168]{3,2,0,1:T(8,128)(2,1)} async-done(((bf16[4,2,40,1792]{3,2,0,1:T(8,128)(2,1)}), bf16[4,2,40,7168]{3,2,0,1:T(8,128)(2,1)}) %all-gather.5.cloned.1.call-update) | async-done | bytes 4587536 | tf_op jit(solution)/shard_map/all_gather | solution.py:59
  120.7 15.7 %fusion.12 = bf16[4,2,40,1024]{3,2,0,1:T(8,128)(2,1)S(1)} fusion(bf16[4,2,40,7168]{3,2,0,1:T(8,128)(2,1)} %all-gather.5.cloned.1.call-done, bf16[1,2,7168,1024]{3,2,1,0:T(8,128)(2,1)} %param.11), kind=kOutput, calls=%fused_computation.8 | convolution fusion | flops 4697948160 | bytes 34603008 | tf_op jit(solution)/shard_map/glcf,lfd->glcd/dot_general | solution.py:60
  136.4 0.0 copy-start.1
  136.4 0.0 copy-start.2
  136.4 0.9 copy.41
  137.3 4.6 %all-to-all-start.1 = ((bf16[4,2,40,1024]{3,2,1,0:T(8,128)(2,1)}), bf16[4,2,40,1024]{3,2,1,0:T(8,128)(2,1)S(1)}, u32[]{:S(2)}, u32[]{:S(2)}) async-start(bf16[4,2,40,1024]{3,2,1,0:T(8,128)(2,1)} %copy.41), calls=%async_computation.1 | async-start | bytes 1310720 | tf_op jit(solution)/shard_map/all_to_all | solution.py:63
  141.9 0.0 copy-done
  141.9 0.0 copy-done.1
  141.9 0.2 fusion.21
  142.1 6.0 %psum.15 = f32[128,8]{0,1:T(8,128)S(1)} all-reduce(f32[128,8]{0,1:T(8,128)S(1)} %fusion.21), channel_id=1, replica_groups=mesh['groups'=2,'expert'=4,'tensor'=4] {'tensor'}, use_global_device_ids=true, to_apply=%region_5.6 | all-reduce | flops 1024 | bytes 8192 | tf_op jit(solution)/shard_map/psum | solution.py:44
  148.2 0.0 copy-done.2
  148.3 11.3 %all-to-all-done.1 = bf16[4,2,40,1024]{3,2,1,0:T(8,128)(2,1)S(1)} async-done(((bf16[4,2,40,1024]{3,2,1,0:T(8,128)(2,1)}), bf16[4,2,40,1024]{3,2,1,0:T(8,128)(2,1)S(1)}, u32[]{:S(2)}, u32[]{:S(2)}) %all-to-all-start.1) | async-done | bytes 655392 | tf_op jit(solution)/shard_map/all_to_all | solution.py:63
  159.6 1.0 convolution_convert_fusion.1
  (9 shorter events, 0.2 us)
Async XLA Ops:
  6.5 135.3 %copy-start = (bf16[4096,8]{0,1:T(8,128)(2,1)S(1)}, bf16[4096,8]{0,1:T(8,128)(2,1)}, u32[]{:S(2)}) copy-start(bf16[4096,8]{0,1:T(8,128)(2,1)} %param.8) | copy-start | bytes 196612
  6.5 61.0 %all-gather.3.cloned.1.call-start = ((), (), s32[]{:S(2)}) async-start(), calls=%async_computation.2 | async-start | bytes 3276800 | tf_op jit(solution)/shard_map/all_gather | solution.py:54
  42.8 77.9 %all-gather.5.cloned.1.call-start = ((), (), s32[]{:S(2)}) async-start(), calls=%async_computation.3 | async-start | bytes 5734400 | tf_op jit(solution)/shard_map/all_gather | solution.py:59
  136.4 5.5 %copy-start.1 = (bf16[128,1024]{1,0:T(8,128)(2,1)S(1)}, bf16[128,1024]{1,0:T(8,128)(2,1)}, u32[]{:S(2)}) copy-start(bf16[128,1024]{1,0:T(8,128)(2,1)} %param.6) | copy-start | bytes 786436
  136.4 11.8 %copy-start.2 = (s32[128,2]{0,1:T(2,128)S(1)}, s32[128,2]{0,1:T(2,128)}, u32[]{:S(2)}) copy-start(s32[128,2]{0,1:T(2,128)} %param.9) | copy-start | bytes 3076
  137.3 22.3 %all-to-all-start.1 = ((bf16[4,2,40,1024]{3,2,1,0:T(8,128)(2,1)}), bf16[4,2,40,1024]{3,2,1,0:T(8,128)(2,1)S(1)}, u32[]{:S(2)}, u32[]{:S(2)}) async-start(bf16[4,2,40,1024]{3,2,1,0:T(8,128)(2,1)} %copy.41), calls=%async_computation.1 | async-start | bytes 1310720 | tf_op jit(solution)/shard_map/all_to_all | solution.py:63
Sparse Core Ops, SparseCore 0:
  42.9 24.6 all-gather.2
  84.0 36.6 all-gather.4
where the time goes:
time: 168 us; the launch traced here: 167 us
  waiting for transfers between devices  72.9 us (43%)
  blocking collectives  35.2 us (21%)
  matrix products  34.5 us (21%)
  between operations  13.5 us (8%)
  starting transfers between devices  4.64 us (3%)
  local copies, waits for them, and re-layouts  3.99 us (2%)
  other arithmetic  2.65 us (2%)
    all_gather x1, waiting for transfers between devices, on_device(): hidden = lax.all_gather(hidden, 'tensor', axis=3, tiled=True)  36.8 us
    all_gather x1, waiting for transfers between devices, on_device(): received = lax.all_gather(received, 'tensor', axis=3, tiled=True)  24.8 us
    all_to_all x1, blocking collectives, on_device(): lax.all_to_all(buffer, 'expert', split_axis=0, concat_axis=0, tiled=True)  20.8 us
    dot_general x1, matrix products, on_device(): jnp.einsum('glcd,ldf->glcf', received, w_gate[0], preferred_element_type=...  16.3 us
    dot_general x1, matrix products, on_device(): jnp.einsum('glcf,lfd->glcd', hidden, w_down[0], preferred_element_type=jn...  15.7 us
    all_to_all x1, waiting for transfers between devices, on_device(): lax.all_to_all(partial_value, 'expert', split_axis=0, concat_axis=0, tile...  11.3 us
    psum x1, blocking collectives, on_device(): squares_sum = lax.psum(jnp.sum(values * values, axis=1), 'tensor')  8.36 us
    psum x1, blocking collectives, on_device(): logits = lax.psum(logit_terms, 'tensor')  6.05 us
  transfers between devices with their start and end apart: 3, of which 3 were waited for; matrix products, arithmetic and copies ran while one was open for 0% of the time, Pallas kernels for 0%

commit v1 on v0

v1 whole, which is shorter than its diff:
```python
import functools

import jax
import jax.numpy as jnp
from jax import lax
from jax.experimental import pallas as pl
from jax.experimental.pallas import tpu as pltpu
from jax.sharding import PartitionSpec as P

CAP = 40
epsilon = 1e-05
MESH = pl.DeviceIdType.MESH
F32 = jnp.float32
BF16 = jnp.bfloat16
NT = (((1,), (1,)), ((), ()))
TN = (((0,), (0,)), ((), ()))


def column_width(width):
    return 256 if width % 256 == 0 else width


def kernel(
    cfg, tok_ref, ids_ref, mix_ref, gain_ref, wg_hbm, wd_hbm, out_ref,
    wg, wd, send_rows, recv, xn, hid, acc, outb, ret, stat, comb, total,
    wg_sem, wd_sem, st_s, st_r, dz_s, dz_r, gx_s, gx_r, gp_s, gp_r,
    hx_s, hx_r, hp_s, hp_r, rz_s, rz_r,
):
    E, T, L, experts, pieces, slots = cfg
    X = T // 2
    e = lax.axis_index("expert")
    t = lax.axis_index("tensor")
    x, c = t // 2, lax.rem(t, 2)
    partner = x * 2 + 1 - c
    W = tok_ref.shape[1]
    rows_t = tok_ref.shape[0]
    NJ, D, cw = wg.shape[1:]
    FW = NJ * cw
    N = acc.shape[1]
    R = E * CAP

    def order(i):
        return lax.rem(e // 2 + i // 2, E // 2) * 2 + lax.rem(e + i, 2)

    def xpeer(k):
        return lax.rem(x + k, X)

    def gate_copy(l, j):
        cols = pl.ds(pl.multiple_of(j * cw, 128), cw) if NJ > 1 else pl.ds(0, cw)
        return pltpu.make_async_copy(wg_hbm.at[0, l, :, cols], wg.at[l, j], wg_sem.at[l, j])

    def peer(i):
        return lax.rem(x + i // 2, X) * 2 + lax.rem(c + i, 2)

    def down_copy(n):
        l, i = n // T, n % T
        rows = pl.ds(pl.multiple_of(peer(i) * FW, 16), FW)
        return pltpu.make_async_copy(wd_hbm.at[0, l, rows, :], wd.at[n % slots], wd_sem.at[n % slots])

    def remote(src, dst, ss, rs, **where):
        return pltpu.make_async_remote_copy(
            src_ref=src, dst_ref=dst, send_sem=ss, recv_sem=rs, device_id=where, device_id_type=MESH
        )

    barrier = pltpu.get_barrier_semaphore()
    for k in range(1, T):
        pl.semaphore_signal(barrier, inc=1, device_id={"tensor": lax.rem(t + k, T)}, device_id_type=MESH)
    for k in range(1, E):
        pl.semaphore_signal(barrier, inc=1, device_id={"expert": lax.rem(e + k, E)}, device_id_type=MESH)

    for l in range(L):
        for j in range(NJ):
            gate_copy(l, j).start()
    for n in range(min(slots, L * T)):
        down_copy(n).start()

    ids0, ids1 = ids_ref[0:1, :], ids_ref[1:2, :]
    label = lax.broadcasted_iota(jnp.int32, (experts, rows_t), 0)
    hot0 = (label == ids0).astype(F32)
    hot1 = (label == ids1).astype(F32)
    earlier = lax.broadcasted_iota(jnp.int32, (rows_t, rows_t), 0) < lax.broadcasted_iota(
        jnp.int32, (rows_t, rows_t), 1
    )
    before = jnp.dot(
        (hot0 + hot1).astype(BF16), earlier.astype(F32).astype(BF16), preferred_element_type=F32
    )
    slot0 = jnp.sum(hot0 * before, axis=0, keepdims=True)
    slot1 = jnp.sum(hot1 * (before + hot0), axis=0, keepdims=True)
    place0 = ids0 * CAP + slot0.astype(jnp.int32)
    place1 = ids1 * CAP + slot1.astype(jnp.int32)

    tokens = tok_ref[...]
    LC = L * CAP
    near = lax.broadcasted_iota(jnp.int32, (LC, rows_t), 0)
    for d in range(E):
        base = near + (d // pieces) * LC
        pick = jnp.where((base == place0) | (base == place1), 1.0, 0.0).astype(BF16)
        send_rows[d] = jnp.dot(pick, tokens, preferred_element_type=F32).astype(BF16)

    pl.semaphore_wait(barrier, T - 1 + E - 1)

    def dz(dest, src):
        return remote(send_rows.at[dest], recv.at[src, t], dz_s.at[dest], dz_r.at[src], expert=dest)

    for i in range(1, E):
        dz(order(i), e).start()
    recv[e, t] = send_rows[e]

    mix = mix_ref[...]
    mix_hi = mix.astype(BF16)
    mix_lo = (mix - mix_hi.astype(F32)).astype(BF16)
    logit = lax.dot_general(mix_hi, tokens, NT, preferred_element_type=F32)
    logit += lax.dot_general(mix_lo, tokens, NT, preferred_element_type=F32)
    sq = tokens.astype(F32) * tokens.astype(F32)
    sq_hi = sq.astype(BF16)
    sq_lo = (sq - sq_hi.astype(F32)).astype(BF16)
    ones = jnp.ones((8, W), BF16)
    squares = lax.dot_general(ones, sq_hi, NT, preferred_element_type=F32)
    squares += lax.dot_general(ones, sq_lo, NT, preferred_element_type=F32)
    stat[t, 0:experts, :] = logit
    stat[t, experts:, :] = squares

    def st(dest, src):
        return remote(stat.at[src], stat.at[src], st_s.at[dest], st_r.at[src], tensor=dest)

    for k in range(1, T):
        st(lax.rem(t + k, T), t).start()

    def gx(s, k):
        to = xpeer(k) * 2 + c
        return remote(recv.at[s, t], recv.at[s, t], gx_s.at[s, xpeer(k)], gx_r.at[s, x], tensor=to)

    def gx_in(s, k):
        q = xpeer(k) * 2 + c
        return remote(recv.at[s, q], recv.at[s, q], gx_s.at[s, xpeer(k)], gx_r.at[s, xpeer(k)], tensor=q)

    def gp(s, k):
        q = xpeer(k) * 2 + c
        return remote(
            recv.at[s, q], recv.at[s, q], gp_s.at[s, xpeer(k)], gp_r.at[s, xpeer(k)], tensor=partner
        )

    def gp_in(s, k):
        q = xpeer(k) * 2 + 1 - c
        return remote(
            recv.at[s, q], recv.at[s, q], gp_s.at[s, xpeer(k)], gp_r.at[s, xpeer(k)], tensor=partner
        )

    def spread(i):
        s = order(i)
        if i > 0:
            dz(s, s).wait_recv()
        for k in range(1, X):
            gx(s, k).start()
        gp(s, 0).start()

    def forward(i):
        s = order(i)
        for k in range(1, X):
            gx_in(s, k).wait_recv()
            gp(s, k).start()

    def arrived(i):
        s = order(i)
        for k in range(X):
            gp_in(s, k).wait_recv()

    def normalize(i):
        first = lax.rem(e // 2 + i // 2, E // 2)
        pair = (first * 2, first * 2 + 1)
        for s in pair:
            pass
        sums = []
        for s in pair:
            square = jnp.zeros((LC, 128), F32)
            for q in range(T):
                v = recv[s, q].astype(F32)
                v = v * v
                for b in range(W // 128):
                    square = square + v[:, b * 128:(b + 1) * 128]
            mean = jnp.sum(square, axis=1, keepdims=True) / D
            sums.append(lax.rsqrt(mean + epsilon))
        rows = pl.ds(pl.multiple_of(first * 2 * CAP, 16), 2 * CAP)
        for q in range(T):
            gain = gain_ref[:, q * W:(q + 1) * W]
            parts = [recv[s, q].astype(F32) * inv * gain for s, inv in zip(pair, sums)]
            for l in range(L):
                block = jnp.concatenate([p[l * CAP:(l + 1) * CAP] for p in parts], axis=0)
                xn[l, rows, q * W:(q + 1) * W] = block.astype(BF16)

    spread(0)

    for k in range(1, T):
        q = lax.rem(t + k, T)
        st(q, q).wait_recv()
    sums = stat[0]
    for q in range(1, T):
        sums = sums + stat[q]
    logits = sums[0:experts] * lax.rsqrt(sums[experts:] / D + epsilon)[0:1]
    chosen0 = jnp.sum(hot0 * logits, axis=0, keepdims=True)
    chosen1 = jnp.sum(hot1 * logits, axis=0, keepdims=True)
    gate0 = (1.0 / (1.0 + jnp.exp(chosen1 - chosen0))).astype(BF16).astype(F32)
    gate1 = (1.0 / (1.0 + jnp.exp(chosen0 - chosen1))).astype(BF16).astype(F32)
    slot_rows = lax.broadcasted_iota(jnp.int32, (CAP, rows_t), 0)
    for d in range(E):
        for l in range(L):
            base = slot_rows + ((d // pieces) * L + l) * CAP
            both = jnp.where(base == place0, gate0, 0.0) + jnp.where(base == place1, gate1, 0.0)
            comb[d, l] = both.astype(BF16)

    for i in range(1, E):
        spread(i)
        forward(i - 1)
        if i % 2 == 0:
            arrived(i - 2)
            arrived(i - 1)
            normalize(i - 2)
    forward(E - 1)
    arrived(E - 2)
    arrived(E - 1)
    normalize(E - 2)

    def hx(l, j, k):
        to = xpeer(k) * 2 + c
        return remote(
            hid.at[l, t, j], hid.at[l, t, j], hx_s.at[l, j, xpeer(k)], hx_r.at[l, j, x], tensor=to
        )

    def hx_in(l, j, k):
        q = xpeer(k) * 2 + c
        return remote(
            hid.at[l, q, j], hid.at[l, q, j], hx_s.at[l, j, xpeer(k)], hx_r.at[l, j, xpeer(k)], tensor=q
        )

    def hp(l, j, k):
        q = xpeer(k) * 2 + c
        return remote(
            hid.at[l, q, j], hid.at[l, q, j], hp_s.at[l, j, xpeer(k)], hp_r.at[l, j, xpeer(k)],
            tensor=partner,
        )

    def hp_in(l, j, k):
        q = xpeer(k) * 2 + 1 - c
        return remote(
            hid.at[l, q, j], hid.at[l, q, j], hp_s.at[l, j, xpeer(k)], hp_r.at[l, j, xpeer(k)],
            tensor=partner,
        )

    def pass_on(l, j):
        for k in range(1, X):
            hx_in(l, j, k).wait_recv()
            hp(l, j, k).start()

    for l in range(L):
        def gate_step(j, carry):
            gate_copy(l, j).wait()
            v = jnp.dot(xn[l], wg[l, j], preferred_element_type=F32)
            hid[l, t, j] = (v * (1.0 / (1.0 + jnp.exp(-v)))).astype(BF16)
            for k in range(1, X):
                hx(l, j, k).start()
            hp(l, j, 0).start()
            if l > 0:
                pass_on(l - 1, j)
            return carry

        lax.fori_loop(0, NJ, gate_step, 0)

    hosts = (L - 1) * T + 2
    passed = 0
    nw = 256 if N % 256 == 0 else N

    def rz(l, dest, src):
        return remote(outb.at[l, dest], ret.at[src, l], rz_s.at[l, dest], rz_r.at[l, src], expert=dest)

    for n in range(L * T):
        l, i = n // T, n % T
        q = peer(i)
        down_copy(n).wait()
        if i > 0:
            k = i // 2
            for j in range(NJ):
                if i % 2 == 1:
                    hp_in(l, j, k).wait_recv()
        slot = n % slots

        def down_step(b, carry):
            cols = pl.ds(pl.multiple_of(b * nw, 128), nw)
            lhs = jnp.concatenate([hid[l, q, j] for j in range(NJ)], axis=1) if NJ > 1 else hid[l, q, 0]
            v = jnp.dot(lhs, wd[slot, :, cols], preferred_element_type=F32)
            if i == 0:
                acc[:, cols] = v
            else:
                acc[:, cols] += v
            return carry

        lax.fori_loop(0, N // nw, down_step, 0)
        if n + slots < L * T:
            down_copy(n + slots).start()
        if n < hosts:
            until = (NJ * (n + 1)) // hosts
            for j in range(passed, until):
                pass_on(L - 1, j)
            passed = until
        if i == T - 1:
            for s in range(E):
                outb[l, s] = acc[s * CAP:(s + 1) * CAP, :].astype(BF16)
            for m in range(1, E):
                rz(l, order(m), e).start()
            ret[e, l] = outb[l, e]

    for l in range(L):
        for m in range(E):
            d = order(m)
            if m > 0:
                rz(l, d, d).wait_recv()
            v = lax.dot_general(comb[d, l], ret[d, l], TN, preferred_element_type=F32)
            if l == 0 and m == 0:
                total[...] = v
            else:
                total[...] += v
    out_ref[...] = total[...].astype(BF16)

    for k in range(1, T):
        st(lax.rem(t + k, T), t).wait_send()
    for i in range(1, E):
        dz(order(i), e).wait_send()
    for i in range(E):
        s = order(i)
        for k in range(1, X):
            gx(s, k).wait_send()
        for k in range(X):
            gp(s, k).wait_send()
    for l in range(L):
        for j in range(NJ):
            for k in range(1, X):
                hx(l, j, k).wait_send()
            for k in range(X):
                hp(l, j, k).wait_send()
        for m in range(1, E):
            rz(l, order(m), e).wait_send()


def on_device(tokens, norm_gain, router, expert_ids, w_gate, w_down):
    rows_t, W = tokens.shape
    experts = router.shape[1]
    E, T = lax.axis_size("expert"), lax.axis_size("tensor")
    L = w_gate.shape[1]
    pieces = max(1, E // experts)
    D = norm_gain.shape[0]
    FW = w_gate.shape[3]
    N = w_down.shape[3]
    cw = column_width(FW)
    NJ = FW // cw
    X = T // 2
    R = E * CAP
    slots = min(6, L * T)
    first = lax.axis_index("tensor") * W
    gain_part = lax.dynamic_slice_in_dim(norm_gain, first, W, 0)
    router_part = lax.dynamic_slice_in_dim(router, first, W, 0)
    mix = (router_part.astype(F32) * gain_part[:, None]).T
    DMA = pltpu.SemaphoreType.DMA
    vmem = pl.BlockSpec(memory_space=pltpu.VMEM)
    hbm = pl.BlockSpec(memory_space=pl.ANY)
    return pl.pallas_call(
        functools.partial(kernel, (E, T, L, experts, pieces, slots)),
        out_shape=jax.ShapeDtypeStruct((rows_t, N), BF16),
        in_specs=[vmem, vmem, vmem, vmem, hbm, hbm],
        out_specs=vmem,
        scratch_shapes=[
            pltpu.VMEM((L, NJ, D, cw), BF16),
            pltpu.VMEM((slots, FW, N), BF16),
            pltpu.VMEM((E, L * CAP, W), BF16),
            pltpu.VMEM((E, T, L * CAP, W), BF16),
            pltpu.VMEM((L, R, D), BF16),
            pltpu.VMEM((L, T, NJ, R, cw), BF16),
            pltpu.VMEM((R, N), F32),
            pltpu.VMEM((L, E, CAP, N), BF16),
            pltpu.VMEM((E, L, CAP, N), BF16),
            pltpu.VMEM((T, experts + 8, rows_t), F32),
            pltpu.VMEM((E, L, CAP, rows_t), BF16),
            pltpu.VMEM((rows_t, N), F32),
            DMA((L, NJ)), DMA((slots,)),
            DMA((T,)), DMA((T,)), DMA((E,)), DMA((E,)),
            DMA((E, X)), DMA((E, X)), DMA((E, X)), DMA((E, X)),
            DMA((L, NJ, X)), DMA((L, NJ, X)), DMA((L, NJ, X)), DMA((L, NJ, X)),
            DMA((L, E)), DMA((L, E)),
        ],
        compiler_params=pltpu.CompilerParams(
            collective_id=0, has_side_effects=True, vmem_limit_bytes=67043328
        ),
    )(tokens, expert_ids.T, mix, norm_gain[None, :], w_gate, w_down)


def solution(mesh):
    return jax.shard_map(
        on_device,
        mesh=mesh,
        in_specs=(
            P(("groups", "expert"), "tensor"),
            P(),
            P(),
            P(("groups", "expert"), None),
            P("expert", None, None, "tensor"),
            P("expert", None, None, "tensor"),
        ),
        out_specs=P(("groups", "expert"), "tensor"),
        check_vma=False,
    )
```

time: 168 us -> 73 us (0.43)
  waiting for transfers between devices: 72.9 us -> 0 us
  Pallas kernels: 0 us -> 69 us
  blocking collectives: 35.2 us -> 0 us
  matrix products: 34.5 us -> 0 us
  between operations: 13.5 us -> 0.01 us
  starting transfers between devices: 4.64 us -> 0 us
    pallas_call x0 -> x1, Pallas kernels: none -> 69 us  [on_device(): pl.pallas_call(functools.partial(kernel, (E, T, L, experts, pieces, slots...]
    all_gather x2 -> x0, waiting for transfers between devices: 61.6 us -> none  [the longest x1 36.8 us: on_device(): hidden = lax.all_gather(hidden, 'tensor', axis=3, tiled=True)]
    dot_general x5 -> x0, matrix products: 34.5 us -> none  [the longest x1 16.3 us: on_device(): jnp.einsum('glcd,ldf->glcf', received, w_gate[0], preferred_element_type=...]
    all_to_all x1 -> x0, blocking collectives: 20.8 us -> none  [on_device(): lax.all_to_all(buffer, 'expert', split_axis=0, concat_axis=0, tiled=True)]
    psum x2 -> x0, blocking collectives: 14.4 us -> none  [the longest x1 8.36 us: on_device(): squares_sum = lax.psum(jnp.sum(values * values, axis=1), 'tensor')]
    all_to_all x1 -> x0, waiting for transfers between devices: 11.3 us -> none  [on_device(): lax.all_to_all(partial_value, 'expert', split_axis=0, concat_axis=0, tile...]
    all_to_all x1 -> x0, starting transfers between devices: 4.6 us -> none  [on_device(): lax.all_to_all(partial_value, 'expert', split_axis=0, concat_axis=0, tile...]
  transfers between devices with their start and end apart: 3 -> 0, of which waited for: 3 -> 0; matrix products, arithmetic and copies ran while one was open for 0% -> 0% of each run, Pallas kernels for 0% -> 0%
where the time goes in v1:
time: 73 us; the launch traced here: 72.7 us
  Pallas kernels  69 us (95%)
  local copies, waits for them, and re-layouts  2.36 us (3%)
  other arithmetic  1.34 us (2%)
    pallas_call x1, Pallas kernels, on_device(): pl.pallas_call(functools.partial(kernel, (E, T, L, experts, pieces, slots...  69 us
    unnamed x1, local copies, waits for them, and re-layouts  1.67 us

profile of v1, /device:TPU:0, one launch (start us, length us, event | category | flops | bytes accessed | tf_op | source)
XLA Modules:
  0.0 72.7 jit_solution(7714112574606906515)
XLA Ops:
  0.0 0.7 dynamic_slice.7
  0.7 1.3 %multiply_bitcast_fusion.mix_ref = f32[8,1024]{1,0:T(8,128)} fusion(f32[1024]{0:T(1024)S(1)} %dynamic_slice.7, bf16[4096,8]{0,1:T(8,128)(2,1)} %param.8, s32[]{:T(128)S(6)} %select_n.4), kind=kLoop, calls=%fused_computation | loop fusion | flops 16384 | bytes 53252 | tf_op jit(solution)/shard_map/transpose | solution.py:360
  2.0 69.0 %shard_map.64 = bf16[128,1024]{1,0:T(8,128)(2,1)} custom-call(bf16[128,1024]{1,0:T(8,128)(2,1)} %tok_ref.1, s32[2,128]{1,0:T(2,128)} %bitcast.5, f32[8,1024]{1,0:T(8,128)} %multiply_bitcast_fusion.mix_ref, f32[1,4096]{1,0:T(1,128)} %bitcast.4, bf16[1,2,4096,1792]{3,2,1,0:T(8,128)(2,1)} %wg_hbm.1, bf16[1,2,7168,1024]{3,2,1,0:T(8,128)(2,1)} %wd_hbm.1), custom_call_target="tpu_custom_call" | custom-call | tf_op jit(solution)/shard_map/pallas_call | solution.py:364
  71.0 1.7 %copy.8 = bf16[128,1024]{1,0:T(8,128)(2,1)} copy(bf16[128,1024]{1,0:T(8,128)(2,1)} %shard_map.64) | data formatting | bytes 524288

commit v2 on v1

--- a/solution.py
+++ b/solution.py
@@ -21,7 +21,7 @@
 
 
 def kernel(
-    cfg, tok_ref, ids_ref, mix_ref, gain_ref, wg_hbm, wd_hbm, out_ref,
+    cfg, tok_ref, ids_ref, router_ref, gain_ref, wg_hbm, wd_hbm, out_ref,
     wg, wd, send_rows, recv, xn, hid, acc, outb, ret, stat, comb, total,
     wg_sem, wd_sem, st_s, st_r, dz_s, dz_r, gx_s, gx_r, gp_s, gp_r,
     hx_s, hx_r, hp_s, hp_r, rz_s, rz_r,
@@ -106,7 +106,8 @@
         dz(order(i), e).start()
     recv[e, t] = send_rows[e]
 
-    mix = mix_ref[...]
+    own = pl.ds(pl.multiple_of(t * W, 128), W)
+    mix = router_ref[:, own].astype(F32) * gain_ref[:, own]
     mix_hi = mix.astype(BF16)
     mix_lo = (mix - mix_hi.astype(F32)).astype(BF16)
     logit = lax.dot_general(mix_hi, tokens, NT, preferred_element_type=F32)
@@ -168,8 +169,6 @@
     def normalize(i):
         first = lax.rem(e // 2 + i // 2, E // 2)
         pair = (first * 2, first * 2 + 1)
-        for s in pair:
-            pass
         sums = []
         for s in pair:
             square = jnp.zeros((LC, 128), F32)
@@ -180,7 +179,7 @@
                     square = square + v[:, b * 128:(b + 1) * 128]
             mean = jnp.sum(square, axis=1, keepdims=True) / D
             sums.append(lax.rsqrt(mean + epsilon))
-        rows = pl.ds(pl.multiple_of(first * 2 * CAP, 16), 2 * CAP)
+        rows = pl.ds(i * CAP, 2 * CAP)
         for q in range(T):
             gain = gain_ref[:, q * W:(q + 1) * W]
             parts = [recv[s, q].astype(F32) * inv * gain for s, inv in zip(pair, sums)]
@@ -208,117 +207,161 @@
             both = jnp.where(base == place0, gate0, 0.0) + jnp.where(base == place1, gate1, 0.0)
             comb[d, l] = both.astype(BF16)
 
-    for i in range(1, E):
+    half_rows = (pl.ds(0, 2 * CAP), pl.ds(2 * CAP, R - 2 * CAP))
+
+    def hid_copy(l, h, j, k, mine, sems, to):
+        block = hid.at[l, xpeer(k) * 2 + (c if mine else 1 - c), j, half_rows[h]]
+        return remote(
+            block, block, sems[0].at[l, j, xpeer(k), h], sems[1].at[l, j, xpeer(k), h], tensor=to
+        )
+
+    def hx(l, h, j, k):
+        block = hid.at[l, t, j, half_rows[h]]
+        return remote(
+            block, block, hx_s.at[l, j, xpeer(k), h], hx_r.at[l, j, x, h], tensor=xpeer(k) * 2 + c
+        )
+
+    def hx_in(l, h, j, k):
+        return hid_copy(l, h, j, k, True, (hx_s, hx_r), xpeer(k) * 2 + c)
+
+    def hp(l, h, j, k):
+        return hid_copy(l, h, j, k, True, (hp_s, hp_r), partner)
+
+    def hp_in(l, h, j, k):
+        return hid_copy(l, h, j, k, False, (hp_s, hp_r), partner)
+
+    def send_hidden(l, h, j):
+        for k in range(1, X):
+            hx(l, h, j, k).start()
+        hp(l, h, j, 0).start()
+
+    def pass_on(l, h, j):
+        for k in range(1, X):
+            hx_in(l, h, j, k).wait_recv()
+            hp(l, h, j, k).start()
+
+    def silu(v):
+        return (v * (1.0 / (1.0 + jnp.exp(-v)))).astype(BF16)
+
+    def near_step(j, carry):
+        gate_copy(0, j).wait()
+        rows = half_rows[0]
+        hid[0, t, j, rows] = silu(jnp.dot(xn[0, rows], wg[0, j], preferred_element_type=F32))
+        send_hidden(0, 0, j)
+        return carry
+
+    def far_step(j, carry):
+        rows = half_rows[1]
+        hid[0, t, j, rows] = silu(jnp.dot(xn[0, rows], wg[0, j], preferred_element_type=F32))
+        send_hidden(0, 1, j)
+        pass_on(0, 0, j)
+        return carry
+
+    spread(1)
+    forward(0)
+    forward(1)
+    spread(2)
+    arrived(0)
+    arrived(1)
+    normalize(0)
+    early = min(3, NJ)
+    lax.fori_loop(0, early, near_step, 0)
+    for i in range(3, E):
         spread(i)
         forward(i - 1)
-        if i % 2 == 0:
-            arrived(i - 2)
-            arrived(i - 1)
-            normalize(i - 2)
+    lax.fori_loop(early, NJ, near_step, 0)
     forward(E - 1)
-    arrived(E - 2)
-    arrived(E - 1)
-    normalize(E - 2)
-
-    def hx(l, j, k):
-        to = xpeer(k) * 2 + c
-        return remote(
-            hid.at[l, t, j], hid.at[l, t, j], hx_s.at[l, j, xpeer(k)], hx_r.at[l, j, x], tensor=to
-        )
-
-    def hx_in(l, j, k):
-        q = xpeer(k) * 2 + c
-        return remote(
-            hid.at[l, q, j], hid.at[l, q, j], hx_s.at[l, j, xpeer(k)], hx_r.at[l, j, xpeer(k)], tensor=q
-        )
-
-    def hp(l, j, k):
-        q = xpeer(k) * 2 + c
-        return remote(
-            hid.at[l, q, j], hid.at[l, q, j], hp_s.at[l, j, xpeer(k)], hp_r.at[l, j, xpeer(k)],
-            tensor=partner,
-        )
-
-    def hp_in(l, j, k):
-        q = xpeer(k) * 2 + 1 - c
-        return remote(
-            hid.at[l, q, j], hid.at[l, q, j], hp_s.at[l, j, xpeer(k)], hp_r.at[l, j, xpeer(k)],
-            tensor=partner,
-        )
-
-    def pass_on(l, j):
-        for k in range(1, X):
-            hx_in(l, j, k).wait_recv()
-            hp(l, j, k).start()
-
-    for l in range(L):
+    for i in range(2, E, 2):
+        arrived(i)
+        arrived(i + 1)
+        normalize(i)
+    lax.fori_loop(0, NJ, far_step, 0)
+
+    for l in range(1, L):
         def gate_step(j, carry):
             gate_copy(l, j).wait()
-            v = jnp.dot(xn[l], wg[l, j], preferred_element_type=F32)
-            hid[l, t, j] = (v * (1.0 / (1.0 + jnp.exp(-v)))).astype(BF16)
-            for k in range(1, X):
-                hx(l, j, k).start()
-            hp(l, j, 0).start()
-            if l > 0:
-                pass_on(l - 1, j)
+            hid[l, t, j] = silu(jnp.dot(xn[l], wg[l, j], preferred_element_type=F32))
+            send_hidden(l, 1, j)
+            pass_on(l - 1, 1, j)
+            if l > 1:
+                pass_on(l - 1, 0, j)
             return carry
 
         lax.fori_loop(0, NJ, gate_step, 0)
 
-    hosts = (L - 1) * T + 2
-    passed = 0
+        def near_send(j, carry):
+            send_hidden(l, 0, j)
+            return carry
+
+        lax.fori_loop(0, NJ, near_send, 0)
+
+    pending = [(L - 1, 1, j) for j in range(NJ)]
+    if L > 1:
+        pending += [(L - 1, 0, j) for j in range(NJ)]
+
+    def drain(count):
+        for _ in range(min(count, len(pending))):
+            pass_on(*pending.pop(0))
+
     nw = 256 if N % 256 == 0 else N
 
     def rz(l, dest, src):
         return remote(outb.at[l, dest], ret.at[src, l], rz_s.at[l, dest], rz_r.at[l, src], expert=dest)
 
-    for n in range(L * T):
-        l, i = n // T, n % T
-        q = peer(i)
-        down_copy(n).wait()
-        if i > 0:
-            k = i // 2
-            for j in range(NJ):
+    groups = [(l, (0, 1)) for l in range(L - 1)] + [(L - 1, (1,)), (L - 1, (0,))]
+    for l, halves in groups:
+        rows = half_rows[halves[0]] if len(halves) == 1 else pl.ds(0, R)
+        for i in range(T):
+            n, q = l * T + i, peer(i)
+            slot = n % slots
+            if halves != (0,):
+                down_copy(n).wait()
+            if i > 0:
+                while any(u[0] == l and u[1] in halves for u in pending) and i > 1:
+                    drain(1)
                 if i % 2 == 1:
-                    hp_in(l, j, k).wait_recv()
-        slot = n % slots
-
-        def down_step(b, carry):
-            cols = pl.ds(pl.multiple_of(b * nw, 128), nw)
-            lhs = jnp.concatenate([hid[l, q, j] for j in range(NJ)], axis=1) if NJ > 1 else hid[l, q, 0]
-            v = jnp.dot(lhs, wd[slot, :, cols], preferred_element_type=F32)
-            if i == 0:
-                acc[:, cols] = v
+                    for h in halves:
+                        for j in range(NJ):
+                            hp_in(l, h, j, i // 2).wait_recv()
+
+            def down_step(b, carry):
+                cols = pl.ds(pl.multiple_of(b * nw, 128), nw)
+                lhs = [hid[l, q, j, rows] for j in range(NJ)]
+                lhs = jnp.concatenate(lhs, axis=1) if NJ > 1 else lhs[0]
+                v = jnp.dot(lhs, wd[slot, :, cols], preferred_element_type=F32)
+                if i == 0:
+                    acc[rows, cols] = v
+                else:
+                    acc[rows, cols] += v
+                return carry
+
+            lax.fori_loop(0, N // nw, down_step, 0)
+            if len(halves) == 2 and n + slots < L * T:
+                down_copy(n + slots).start()
+            if halves != (0,):
+                drain(NJ * (i + 1) // T - NJ * i // T)
+        out_of = [m for h in halves for m in (range(2) if h == 0 else range(2, E))]
+        for m in out_of:
+            s = lax.rem(e // 2 + m // 2, E // 2) * 2 + m % 2
+            outb[l, s] = acc[m * CAP:(m + 1) * CAP, :].astype(BF16)
+        for m in out_of:
+            if m > 0:
+                rz(l, order(m), e).start()
             else:
-                acc[:, cols] += v
-            return carry
-
-        lax.fori_loop(0, N // nw, down_step, 0)
-        if n + slots < L * T:
-            down_copy(n + slots).start()
-        if n < hosts:
-            until = (NJ * (n + 1)) // hosts
-            for j in range(passed, until):
-                pass_on(L - 1, j)
-            passed = until
-        if i == T - 1:
-            for s in range(E):
-                outb[l, s] = acc[s * CAP:(s + 1) * CAP, :].astype(BF16)
-            for m in range(1, E):
-                rz(l, order(m), e).start()
-            ret[e, l] = outb[l, e]
-
-    for l in range(L):
-        for m in range(E):
-            d = order(m)
-            if m > 0:
-                rz(l, d, d).wait_recv()
-            v = lax.dot_general(comb[d, l], ret[d, l], TN, preferred_element_type=F32)
-            if l == 0 and m == 0:
-                total[...] = v
-            else:
-                total[...] += v
-    out_ref[...] = total[...].astype(BF16)
+                ret[e, l] = outb[l, e]
+
+    returns = [(l, m) for l in range(L - 1) for m in range(E)]
+    returns += [(L - 1, m) for m in list(range(2, E)) + [0, 1]]
+    for l, m in returns:
+        d = order(m)
+        if m > 0:
+            rz(l, d, d).wait_recv()
+        v = lax.dot_general(comb[d, l], ret[d, l], TN, preferred_element_type=F32)
+        if (l, m) == returns[0]:
+            total[...] = v
+        else:
+            total[...] += v
+    out_ref[...] = total[...]
 
     for k in range(1, T):
         st(lax.rem(t + k, T), t).wait_send()
@@ -332,10 +375,11 @@
             gp(s, k).wait_send()
     for l in range(L):
         for j in range(NJ):
-            for k in range(1, X):
-                hx(l, j, k).wait_send()
-            for k in range(X):
-                hp(l, j, k).wait_send()
+            for h in range(2):
+                for k in range(1, X):
+                    hx(l, h, j, k).wait_send()
+                for k in range(X):
+                    hp(l, h, j, k).wait_send()
         for m in range(1, E):
             rz(l, order(m), e).wait_send()
 
@@ -353,17 +397,13 @@
     NJ = FW // cw
     X = T // 2
     R = E * CAP
-    slots = min(6, L * T)
-    first = lax.axis_index("tensor") * W
-    gain_part = lax.dynamic_slice_in_dim(norm_gain, first, W, 0)
-    router_part = lax.dynamic_slice_in_dim(router, first, W, 0)
-    mix = (router_part.astype(F32) * gain_part[:, None]).T
+    slots = min(T + 2, L * T)
     DMA = pltpu.SemaphoreType.DMA
     vmem = pl.BlockSpec(memory_space=pltpu.VMEM)
     hbm = pl.BlockSpec(memory_space=pl.ANY)
     return pl.pallas_call(
         functools.partial(kernel, (E, T, L, experts, pieces, slots)),
-        out_shape=jax.ShapeDtypeStruct((rows_t, N), BF16),
+        out_shape=jax.ShapeDtypeStruct((rows_t, N), F32),
         in_specs=[vmem, vmem, vmem, vmem, hbm, hbm],
         out_specs=vmem,
         scratch_shapes=[
@@ -382,13 +422,13 @@
             DMA((L, NJ)), DMA((slots,)),
             DMA((T,)), DMA((T,)), DMA((E,)), DMA((E,)),
             DMA((E, X)), DMA((E, X)), DMA((E, X)), DMA((E, X)),
-            DMA((L, NJ, X)), DMA((L, NJ, X)), DMA((L, NJ, X)), DMA((L, NJ, X)),
+            DMA((L, NJ, X, 2)), DMA((L, NJ, X, 2)), DMA((L, NJ, X, 2)), DMA((L, NJ, X, 2)),
             DMA((L, E)), DMA((L, E)),
         ],
         compiler_params=pltpu.CompilerParams(
             collective_id=0, has_side_effects=True, vmem_limit_bytes=67043328
         ),
-    )(tokens, expert_ids.T, mix, norm_gain[None, :], w_gate, w_down)
+    )(tokens, expert_ids.T, router.T, norm_gain[None, :], w_gate, w_down).astype(BF16)
 
 
 def solution(mesh):

time: 73 us -> 67.5 us (0.925)
  Pallas kernels: 69 us -> 65.5 us
  local copies, waits for them, and re-layouts: 2.36 us -> 0 us
    pallas_call x1, Pallas kernels: 69 us -> 65.5 us  [on_device(): pl.pallas_call(functools.partial(kernel, (E, T, L, experts, pieces, slots...]
    convert_element_type x0 -> x1, other arithmetic: none -> 1.78 us  [on_device(): return pl.pallas_call(functools.partial(kernel, (E, T, L, experts, pieces...]
    unnamed x1 -> x0, local copies, waits for them, and re-layouts: 1.67 us -> none
    transpose x1 -> x0, other arithmetic: 1.34 us -> none  [on_device(): mix = (router_part.astype(F32) * gain_part[:, None]).T]
where the time goes in v2:
time: 67.5 us; the launch traced here: 67.3 us
  Pallas kernels  65.5 us (97%)
  other arithmetic  1.78 us (3%)
    pallas_call x1, Pallas kernels, on_device(): pl.pallas_call(functools.partial(kernel, (E, T, L, experts, pieces, slots...  65.5 us
    convert_element_type x1, other arithmetic, on_device(): return pl.pallas_call(functools.partial(kernel, (E, T, L, experts, pieces...  1.78 us

profile of v2, /device:TPU:0, one launch (start us, length us, event | category | flops | bytes accessed | tf_op | source)
XLA Modules:
  0.0 67.3 jit_solution(8406677259817100196)
XLA Ops:
  0.0 65.5 %shard_map.64 = f32[128,1024]{1,0:T(8,128)} custom-call(bf16[128,1024]{1,0:T(8,128)(2,1)} %tok_ref.1, s32[2,128]{1,0:T(2,128)} %bitcast.5, bf16[8,4096]{1,0:T(8,128)(2,1)} %bitcast.3, f32[1,4096]{1,0:T(1,128)} %bitcast.4, bf16[1,2,4096,1792]{3,2,1,0:T(8,128)(2,1)} %wg_hbm.1, bf16[1,2,7168,1024]{3,2,1,0:T(8,128)(2,1)} %wd_hbm.1), custom_call_target="tpu_custom_call" | custom-call | tf_op jit(solution)/shard_map/pallas_call | solution.py:404
  65.5 1.8 %convert_element_type.3 = bf16[128,1024]{1,0:T(8,128)(2,1)} convert(f32[128,1024]{1,0:T(8,128)} %shard_map.64) | non-fusion elementwise | flops 131072 | bytes 786432 | tf_op jit(solution)/shard_map/convert_element_type | solution.py:431

commit v3 on v2

--- a/solution.py
+++ b/solution.py
@@ -303,7 +303,7 @@
         for _ in range(min(count, len(pending))):
             pass_on(*pending.pop(0))
 
-    nw = 256 if N % 256 == 0 else N
+    nw = 512 if N % 512 == 0 else N
 
     def rz(l, dest, src):
         return remote(outb.at[l, dest], ret.at[src, l], rz_s.at[l, dest], rz_r.at[l, src], expert=dest)

time: 67.5 us -> 66.6 us (0.987)
  Pallas kernels: 65.5 us -> 64.6 us
    pallas_call x1, Pallas kernels: 65.5 us -> 64.6 us  [on_device(): pl.pallas_call(functools.partial(kernel, (E, T, L, experts, pieces, slots...]
where the time goes in v3:
time: 66.6 us; the launch traced here: 66.4 us
  Pallas kernels  64.6 us (97%)
  other arithmetic  1.78 us (3%)
    pallas_call x1, Pallas kernels, on_device(): pl.pallas_call(functools.partial(kernel, (E, T, L, experts, pieces, slots...  64.6 us
    convert_element_type x1, other arithmetic, on_device(): return pl.pallas_call(functools.partial(kernel, (E, T, L, experts, pieces...  1.78 us

profile of v3, /device:TPU:0, one launch (start us, length us, event | category | flops | bytes accessed | tf_op | source)
XLA Modules:
  0.0 66.4 jit_solution(13605890796850615959)
XLA Ops:
  0.0 64.6 %shard_map.64 = f32[128,1024]{1,0:T(8,128)} custom-call(bf16[128,1024]{1,0:T(8,128)(2,1)} %tok_ref.1, s32[2,128]{1,0:T(2,128)} %bitcast.5, bf16[8,4096]{1,0:T(8,128)(2,1)} %bitcast.3, f32[1,4096]{1,0:T(1,128)} %bitcast.4, bf16[1,2,4096,1792]{3,2,1,0:T(8,128)(2,1)} %wg_hbm.1, bf16[1,2,7168,1024]{3,2,1,0:T(8,128)(2,1)} %wd_hbm.1), custom_call_target="tpu_custom_call" | custom-call | tf_op jit(solution)/shard_map/pallas_call | solution.py:404
  64.6 1.8 %convert_element_type.3 = bf16[128,1024]{1,0:T(8,128)(2,1)} convert(f32[128,1024]{1,0:T(8,128)} %shard_map.64) | non-fusion elementwise | flops 131072 | bytes 786432 | tf_op jit(solution)/shard_map/convert_element_type | solution.py:431
